TPU v7x, 32 devices: a whole 2x2x4 slice. The times are simulated.
32 devices in a mesh: sub: 8 (over y, x, core), reg: 4 (over z).
Axes of the slice: x: 2, y: 2, z: 4, core: 2. Of those that a mesh axis runs over, the one named last changes fastest.
Arguments:
- right_side: float32 [8, 4, 1280, 16], P('sub', 'reg'), may hold values from -6 to 6
- tiles: bfloat16 [8, 4, 80, 128, 128], P('sub', 'reg'), may hold values from -1 to 5
- tile_list: int32 [8, 4, 80, 2], P('sub', 'reg'), may hold values from 0 to 9, as said below
- weights: float32 [8, 4, 1280], P('sub', 'reg'), may hold values from 0.15 to 0.35
- face_map: int32 [8, 4, 6], P('sub', 'reg'), may hold values from 0 to 9, as said below
- matching: int32 [8, 4, 6, 128], P('sub', 'reg'), may hold values from 0 to 127, each once within a row
- coarse_basis: bfloat16 [8, 4, 1280, 128], P('sub', 'reg'), may hold values from -0.15625 to 0.15625
- coarse_map: int32 [8, 4, 128], P('sub', 'reg'), may hold values from 0 to 511, as said below
- coarse_inverse: float32 [4, 512, 512], P('reg', 'sub'), may hold values from -1 to 2, as said below
Outputs:
- solution: bfloat16 [8, 4, 1280, 16], P('sub', 'reg')
- residual: bfloat16 [8, 4, 1280, 16], P('sub', 'reg')
Inputs may be any that keep to these rules, and one draw needn't show every extreme that they name: `tile_list`: entries 0 to 9 of each subdomain's list are (b, b) for b in order; the other 70 entries are distinct off-diagonal block pairs. `face_map`: the six blocks of a subdomain are distinct. `coarse_map`: A subdomain's 128 numbers are distinct, and within a subregion every number is named by exactly two subdomains. `coarse_inverse`: symmetric in its last two dimensions.
All inputs are finite; a program needn't handle non-finite values.
Results may differ from a plain program's by a relative error of at most 0.0075.
Values may be sent and summed in bfloat16 or wider, within the bound.
No kernel may reach another device: no remote copies, remote signals or barrier semaphores. Data moves between devices by JAX's collectives and lax.ppermute only.
A program may use at most 64 MiB of HBM per device.

v0:
```python
import jax
import jax.numpy as jnp
from jax import lax
from jax.sharding import PartitionSpec as P

SWEEPS = 3


def from_behind(shard, axis, by):
    peers = lax.axis_size(axis)
    return lax.ppermute(shard, axis, [(i, (i + by) % peers) for i in range(peers)])


def body(
    right_side,
    tiles,
    tile_list,
    weights,
    face_map,
    matching,
    coarse_basis,
    coarse_map,
    coarse_inverse,
):
    order = right_side.shape[2]
    rights = right_side.shape[3]
    tile = tiles.shape[3]
    blocks = order // tile
    target = right_side[0, 0]
    tile_block = tiles[0, 0]
    listing = tile_list[0, 0]
    scaling = weights[0, 0][:, None]
    faces_here = face_map[0, 0]
    matched = matching[0, 0]
    basis = coarse_basis[0, 0]
    own_map = coarse_map[0, 0]
    own_count = own_map.shape[0]
    inverse_rows = coarse_inverse[0]
    held_rows = inverse_rows.shape[0]
    block_ids = jnp.arange(blocks, dtype=jnp.int32)
    row_table = (listing[:, 0][None, :] == block_ids[:, None]).astype(jnp.float32)
    face_table = (faces_here[None, :] == block_ids[:, None]).astype(jnp.float32)
    stride = max(lax.axis_size("reg") // 4, 1)
    every_ids = lax.all_gather(own_map, "sub", axis=0, tiled=True)
    outgoing_part = jnp.take(inverse_rows, every_ids, axis=1).reshape(
        held_rows, lax.axis_size("sub"), own_count
    )
    received_part = lax.all_to_all(outgoing_part, "sub", split_axis=1, concat_axis=0, tiled=True)
    own_columns = received_part.reshape(held_rows * lax.axis_size("sub"), own_count)
    own_block = jnp.transpose(jnp.take(own_columns, every_ids, axis=0))
    solution = jnp.zeros_like(target)
    residual = target
    for sweep in range(SWEEPS):
        low = residual.astype(jnp.bfloat16)
        local_coarse = jnp.einsum("mn,mr->nr", basis, low, preferred_element_type=jnp.float32)
        own_solution = jnp.dot(
            own_block,
            lax.all_gather(local_coarse, "sub", axis=0, tiled=True),
            precision=lax.Precision.HIGHEST,
            preferred_element_type=jnp.float32,
        )
        own_values = own_solution.astype(jnp.bfloat16)
        correction = jnp.dot(basis, own_values, preferred_element_type=jnp.float32)
        solution = solution + (scaling * residual + correction)
        operator_low = solution.astype(jnp.bfloat16).reshape(blocks, tile, rights)
        picked = jnp.take(operator_low, listing[:, 1], axis=0)
        products = jnp.einsum(
            "tij,tjr->tir", tile_block, picked, preferred_element_type=jnp.float32
        )
        local = jnp.einsum("bt,tir->bir", row_table, products, precision=lax.Precision.HIGHEST)
        stacked = solution.reshape(blocks, tile, rights)
        outgoing = jnp.take(stacked, faces_here, axis=0)
        arrived = []
        for face, offset in ((0, 1), (1, -1), (2, stride), (3, -stride)):
            arrived.append(from_behind(outgoing[face ^ 1], "reg", offset))
        for face, offset in ((4, 1), (5, -1)):
            arrived.append(from_behind(outgoing[face ^ 1], "sub", offset))
        received = jnp.stack(arrived)
        permuted = jnp.take_along_axis(received, matched[:, :, None], axis=1)
        coupling = jnp.einsum("bk,kir->bir", face_table, permuted, precision=lax.Precision.HIGHEST)
        residual = target - (local - 0.5 * coupling).reshape(order, rights)
    shape = (1, 1, order, rights)
    return (
        solution.astype(jnp.bfloat16).reshape(shape),
        residual.astype(jnp.bfloat16).reshape(shape),
    )


def solution(mesh):
    placed = (
        P("sub", "reg", None, None),
        P("sub", "reg", None, None, None),
        P("sub", "reg", None, None),
        P("sub", "reg", None),
        P("sub", "reg", None),
        P("sub", "reg", None, None),
        P("sub", "reg", None, None),
        P("sub", "reg", None),
        P("reg", "sub", None),
    )
    return jax.shard_map(
        body,
        mesh=mesh,
        in_specs=placed,
        out_specs=(P("sub", "reg", None, None), P("sub", "reg", None, None)),
        check_vma=False,
    )
```

profile of v0, /device:TPU:0, one launch (start us, length us, event | category | flops | bytes accessed | tf_op | source)
XLA Modules:
  0.0 149.0 jit_solution(13466135424913627133)
XLA Ops:
  0.7 10.7 %all-gather = s32[1,1,1024]{2,1,0:T(1,128)S(1)} all-gather(s32[1,1,128]{2,1,0:T(1,128)} %param.22), channel_id=2, replica_groups=mesh['sub'=8,'reg'=4] {'sub'}, dimensions={2}, use_global_device_ids=true | all-gather | bytes 4608 | tf_op jit(solution)/shard_map/all_gather | solution.py:44
  12.4 4.0 %gather_fusion = f32[1024,64]{1,0:T(8,128)} fusion(f32[64,512]{0,1:T(8,128)S(1)} %bitcast.251, s32[1024]{0:T(1024)S(1)} %fusion.82), kind=kCustom, calls=%fused_computation.9 | custom fusion | bytes 528384 | tf_op jit(solution)/shard_map/jit(_take)/gather | solution.py:45
  18.3 3.4 %all-to-all-start = ((f32[64,8,128]{2,0,1:T(8,128)}), f32[64,8,128]{2,0,1:T(8,128)S(1)}, u32[]{:S(2)}, u32[]{:S(2)}) async-start(f32[64,8,128]{2,0,1:T(8,128)} %broadcast_select_fusion), calls=%async_computation | async-start | bytes 524288 | tf_op jit(solution)/shard_map/all_to_all | solution.py:48
  23.7 9.5 %all_gather.13 = f32[1024,16]{0,1:T(8,128)S(1)} all-gather(f32[128,16]{0,1:T(8,128)S(1)} %fusion.37), channel_id=1, replica_groups=mesh['sub'=8,'reg'=4] {'sub'}, dimensions={0}, use_global_device_ids=true | all-gather | bytes 73728 | tf_op jit(solution)/shard_map/all_gather | solution.py:58
  33.3 4.0 %gather_fusion.1 = f32[1024,128]{1,0:T(8,128)} fusion(f32[512,128]{1,0:T(8,128)S(1)} %bitcast.250, s32[1024]{0:T(1024)S(1)} %fusion.82), kind=kCustom, calls=%fused_computation.10 | custom fusion | bytes 1052672 | tf_op jit(solution)/shard_map/jit(_take)/gather | solution.py:50
  39.7 1.6 %collective-permute-start = (f32[128,16]{0,1:T(8,128)S(1)}, f32[128,16]{0,1:T(8,128)}, u32[]{:S(2)}, u32[]{:S(2)}) collective-permute-start(f32[128,16]{0,1:T(8,128)S(1)} %get-tuple-element.26), channel_id=1, source_target_pairs={{0,1},{1,2},{2,3},{3,0},{4,5},{5,6},{6,7},{7,4},{8,9},{9,10},{10,1... | collective-permute-start | bytes 24584 | tf_op jit(solution)/shard_map/ppermute | solution.py:11
  41.3 2.2 %collective-permute-start.1 = (f32[128,16]{0,1:T(8,128)S(1)}, f32[128,16]{0,1:T(8,128)}, u32[]{:S(2)}, u32[]{:S(2)}) collective-permute-start(f32[128,16]{0,1:T(8,128)S(1)} %get-tuple-element.25), channel_id=1, source_target_pairs={{0,3},{1,0},{2,1},{3,2},{4,7},{5,4},{6,5},{7,6},{8,11},{9,8},{10,9... | collective-permute-start | bytes 24584 | tf_op jit(solution)/shard_map/ppermute | solution.py:11
  43.6 3.8 %collective-permute-start.3 = (f32[128,16]{0,1:T(8,128)S(1)}, f32[128,16]{0,1:T(8,128)}, u32[]{:S(2)}, u32[]{:S(2)}) collective-permute-start(f32[128,16]{0,1:T(8,128)S(1)} %get-tuple-element.23), channel_id=1, source_target_pairs={{0,3},{1,0},{2,1},{3,2},{4,7},{5,4},{6,5},{7,6},{8,11},{9,8},{10,9... | collective-permute-start | bytes 24584 | tf_op jit(solution)/shard_map/ppermute | solution.py:11
  48.2 2.2 %fusion.11 = f32[80,128,16]{1,2,0:T(8,128)S(1)} fusion(bf16[1,1,80,128,128]{4,3,2,1,0:T(8,128)(2,1)S(1)} %copy-done, bf16[80,128,16]{1,2,0:T(8,128)(2,1)S(1)} %gather_fusion.2, pred[80]{0:T(512)(128)(4,1)} %get-tuple-element.4), kind=kOutput, calls=%fused_computation.25 | convolution fusion | flops 42106880 | bytes 3604560 | tf_op jit(solution)/shard_map/tij,tjr->tir/dot_general | solution.py:67
  51.5 2.6 %collective-permute-start.5 = (f32[128,16]{0,1:T(8,128)S(1)}, f32[128,16]{0,1:T(8,128)S(1)}, u32[]{:S(2)}, u32[]{:S(2)}) collective-permute-start(f32[128,16]{0,1:T(8,128)S(1)} %get-tuple-element.21), channel_id=1, source_target_pairs={{0,28},{4,0},{8,4},{12,8},{16,12},{20,16},{24,20},{28,24},{1,29},{... | collective-permute-start | bytes 24584 | tf_op jit(solution)/shard_map/ppermute | solution.py:11
  62.2 7.0 %gather_fusion.4 = f32[768,16]{1,0:T(8,128)} fusion(f32[6,128,16]{2,1,0:T(8,128)S(1)} %copy.35, s32[768]{0:T(1024)S(1)} %bitcast.246), kind=kCustom, calls=%fused_computation.2.clone | custom fusion | bytes 104448 | tf_op jit(solution)/shard_map/jit(take_along_axis)/gather | solution.py:79
  71.8 9.0 %all_gather.14 = f32[1024,16]{0,1:T(8,128)S(1)} all-gather(f32[128,16]{0,1:T(8,128)S(1)} %convolution_bitcast_fusion.4), channel_id=1, replica_groups=mesh['sub'=8,'reg'=4] {'sub'}, dimensions={0}, use_global_device_ids=true | all-gather | bytes 73728 | tf_op jit(solution)/shard_map/all_gather | solution.py:58
  84.2 2.4 %fusion.14 = f32[80,128,16]{1,2,0:T(8,128)} fusion(bf16[1,1,80,128,128]{4,3,2,1,0:T(8,128)(2,1)S(1)} %copy-done, bf16[80,128,16]{1,2,0:T(8,128)(2,1)S(1)} %gather_fusion.5, pred[80]{0:T(512)(128)(4,1)S(1)} %copy-done.13), kind=kOutput, calls=%fused_computation.26 | convolution fusion | flops 42106880 | bytes 3604560 | tf_op jit(solution)/shard_map/tij,tjr->tir/dot_general | solution.py:67
  87.3 2.2 %fusion.25 = f32[10,128,16]{1,0,2:T(8,128)} fusion(f32[80,128,16]{1,2,0:T(8,128)} %fusion.14, s32[80]{0:T(128)S(1)} %copy-done.12), kind=kOutput, calls=%fused_computation.41 | convolution fusion | flops 19661600 | bytes 737600 | tf_op jit(solution)/shard_map/bt,tir->bir/dot_general | solution.py:70
  89.5 3.8 %collective-permute-start.7 = (f32[128,16]{0,1:T(8,128)S(1)}, f32[128,16]{0,1:T(8,128)S(1)}, u32[]{:S(2)}, u32[]{:S(2)}) collective-permute-start(f32[128,16]{0,1:T(8,128)S(1)} %get-tuple-element.19), channel_id=1, source_target_pairs={{0,3},{1,0},{2,1},{3,2},{4,7},{5,4},{6,5},{7,6},{8,11},{9,8},{10,9... | collective-permute-start | bytes 24584 | tf_op jit(solution)/shard_map/ppermute | solution.py:11
  93.3 3.8 %collective-permute-start.9 = (f32[128,16]{0,1:T(8,128)S(1)}, f32[128,16]{0,1:T(8,128)S(1)}, u32[]{:S(2)}, u32[]{:S(2)}) collective-permute-start(f32[128,16]{0,1:T(8,128)S(1)} %get-tuple-element.17), channel_id=1, source_target_pairs={{0,3},{1,0},{2,1},{3,2},{4,7},{5,4},{6,5},{7,6},{8,11},{9,8},{10,9... | collective-permute-start | bytes 24584 | tf_op jit(solution)/shard_map/ppermute | solution.py:11
  97.1 2.6 %collective-permute-start.11 = (f32[128,16]{0,1:T(8,128)S(1)}, f32[128,16]{0,1:T(8,128)S(1)}, u32[]{:S(2)}, u32[]{:S(2)}) collective-permute-start(f32[128,16]{0,1:T(8,128)S(1)} %get-tuple-element.15), channel_id=1, source_target_pairs={{0,28},{4,0},{8,4},{12,8},{16,12},{20,16},{24,20},{28,24},{1,29},{... | collective-permute-start | bytes 24584 | tf_op jit(solution)/shard_map/ppermute | solution.py:11
  101.3 7.0 %gather_fusion.7 = f32[768,16]{1,0:T(8,128)} fusion(f32[6,128,16]{2,1,0:T(8,128)S(1)} %copy.40, s32[768]{0:T(1024)S(1)} %bitcast.247), kind=kCustom, calls=%fused_computation.7.clone | custom fusion | bytes 104448 | tf_op jit(solution)/shard_map/jit(take_along_axis)/gather | solution.py:79
  110.9 9.3 %all_gather.15 = f32[1024,16]{0,1:T(8,128)S(1)} all-gather(f32[128,16]{0,1:T(8,128)S(1)} %convolution_bitcast_fusion.3), channel_id=1, replica_groups=mesh['sub'=8,'reg'=4] {'sub'}, dimensions={0}, use_global_device_ids=true | all-gather | bytes 73728 | tf_op jit(solution)/shard_map/all_gather | solution.py:58
  123.4 2.4 %fusion.17 = f32[80,128,16]{1,2,0:T(8,128)} fusion(bf16[1,1,80,128,128]{4,3,2,1,0:T(8,128)(2,1)S(1)} %copy-done, bf16[80,128,16]{1,2,0:T(8,128)(2,1)S(1)} %gather_fusion.8, pred[80]{0:T(512)(128)(4,1)S(1)} %copy-done.13), kind=kOutput, calls=%fused_computation.27 | convolution fusion | flops 42106880 | bytes 3604560 | tf_op jit(solution)/shard_map/tij,tjr->tir/dot_general | solution.py:67
  128.0 3.9 %collective-permute-start.13 = (f32[128,16]{0,1:T(8,128)S(1)}, f32[128,16]{0,1:T(8,128)S(1)}, u32[]{:S(2)}, u32[]{:S(2)}) collective-permute-start(f32[128,16]{0,1:T(8,128)S(1)} %get-tuple-element.13), channel_id=1, source_target_pairs={{0,3},{1,0},{2,1},{3,2},{4,7},{5,4},{6,5},{7,6},{8,11},{9,8},{10,9... | collective-permute-start | bytes 24584 | tf_op jit(solution)/shard_map/ppermute | solution.py:11
  131.9 3.8 %collective-permute-start.15 = (f32[128,16]{0,1:T(8,128)S(1)}, f32[128,16]{0,1:T(8,128)S(1)}, u32[]{:S(2)}, u32[]{:S(2)}) collective-permute-start(f32[128,16]{0,1:T(8,128)S(1)} %get-tuple-element.11), channel_id=1, source_target_pairs={{0,3},{1,0},{2,1},{3,2},{4,7},{5,4},{6,5},{7,6},{8,11},{9,8},{10,9... | collective-permute-start | bytes 24584 | tf_op jit(solution)/shard_map/ppermute | solution.py:11
  135.7 2.6 %collective-permute-start.17 = (f32[128,16]{0,1:T(8,128)S(1)}, f32[128,16]{0,1:T(8,128)S(1)}, u32[]{:S(2)}, u32[]{:S(2)}) collective-permute-start(f32[128,16]{0,1:T(8,128)S(1)} %get-tuple-element.9), channel_id=1, source_target_pairs={{0,28},{4,0},{8,4},{12,8},{16,12},{20,16},{24,20},{28,24},{1,29},{... | collective-permute-start | bytes 24584 | tf_op jit(solution)/shard_map/ppermute | solution.py:11
  139.9 7.0 %gather_fusion.10 = f32[768,16]{1,0:T(8,128)} fusion(f32[6,128,16]{2,1,0:T(8,128)S(1)} %copy.45, s32[768]{0:T(1024)S(1)} %bitcast.248), kind=kCustom, calls=%fused_computation.8.clone | custom fusion | bytes 104448 | tf_op jit(solution)/shard_map/jit(take_along_axis)/gather | solution.py:79
  (133 shorter events, 37.1 us)
Async XLA Ops:
  0.6 47.6 %copy-start = (bf16[1,1,80,128,128]{4,3,2,1,0:T(8,128)(2,1)S(1)}, bf16[1,1,80,128,128]{4,3,2,1,0:T(8,128)(2,1)}, u32[]{:S(2)}) copy-start(bf16[1,1,80,128,128]{4,3,2,1,0:T(8,128)(2,1)} %param.16) | copy-start | bytes 7864324
  0.7 22.2 %copy-start.5 = (s32[1,1,6,128]{3,1,2,0:T(1,128)S(1)}, s32[1,1,6,128]{3,1,2,0:T(1,128)}, u32[]{:S(2)}) copy-start(s32[1,1,6,128]{3,1,2,0:T(1,128)} %param.20) | copy-start | bytes 9220
  0.7 22.2 %copy-start.1 = (bf16[1,1,1280,128]{3,2,1,0:T(8,128)(2,1)S(1)}, bf16[1,1,1280,128]{3,2,1,0:T(8,128)(2,1)}, u32[]{:S(2)}) copy-start(bf16[1,1,1280,128]{3,2,1,0:T(8,128)(2,1)} %param.21) | copy-start | bytes 983044
  0.7 22.2 %copy-start.2 = (f32[1,1,1280,16]{2,3,1,0:T(8,128)S(1)}, f32[1,1,1280,16]{2,3,1,0:T(8,128)}, u32[]{:S(2)}) copy-start(f32[1,1,1280,16]{2,3,1,0:T(8,128)} %param.15) | copy-start | bytes 245764
  0.7 32.5 %copy-start.6 = (f32[1,1,1280]{2,1,0:T(1,128)S(1)}, f32[1,1,1280]{2,1,0:T(1,128)}, u32[]{:S(2)}) copy-start(f32[1,1,1280]{2,1,0:T(1,128)} %param.18) | copy-start | bytes 15364
  18.3 14.9 %all-to-all-start = ((f32[64,8,128]{2,0,1:T(8,128)}), f32[64,8,128]{2,0,1:T(8,128)S(1)}, u32[]{:S(2)}, u32[]{:S(2)}) async-start(f32[64,8,128]{2,0,1:T(8,128)} %broadcast_select_fusion), calls=%async_computation | async-start | bytes 524288 | tf_op jit(solution)/shard_map/all_to_all | solution.py:48
  39.7 11.8 %collective-permute-start = (f32[128,16]{0,1:T(8,128)S(1)}, f32[128,16]{0,1:T(8,128)}, u32[]{:S(2)}, u32[]{:S(2)}) collective-permute-start(f32[128,16]{0,1:T(8,128)S(1)} %get-tuple-element.26), channel_id=1, source_target_pairs={{0,1},{1,2},{2,3},{3,0},{4,5},{5,6},{6,7},{7,4},{8,9},{9,10},{10,1... | collective-permute-start | bytes 24584 | tf_op jit(solution)/shard_map/ppermute | solution.py:11
  41.3 14.2 %collective-permute-start.1 = (f32[128,16]{0,1:T(8,128)S(1)}, f32[128,16]{0,1:T(8,128)}, u32[]{:S(2)}, u32[]{:S(2)}) collective-permute-start(f32[128,16]{0,1:T(8,128)S(1)} %get-tuple-element.25), channel_id=1, source_target_pairs={{0,3},{1,0},{2,1},{3,2},{4,7},{5,4},{6,5},{7,6},{8,11},{9,8},{10,9... | collective-permute-start | bytes 24584 | tf_op jit(solution)/shard_map/ppermute | solution.py:11
  43.6 13.2 %collective-permute-start.2 = (f32[128,16]{0,1:T(8,128)S(1)}, f32[128,16]{0,1:T(8,128)}, u32[]{:S(2)}, u32[]{:S(2)}) collective-permute-start(f32[128,16]{0,1:T(8,128)S(1)} %get-tuple-element.24), channel_id=1, source_target_pairs={{0,1},{1,2},{2,3},{3,0},{4,5},{5,6},{6,7},{7,4},{8,9},{9,10},{10,1... | collective-permute-start | bytes 24584 | tf_op jit(solution)/shard_map/ppermute | solution.py:11
  43.6 14.5 %collective-permute-start.3 = (f32[128,16]{0,1:T(8,128)S(1)}, f32[128,16]{0,1:T(8,128)}, u32[]{:S(2)}, u32[]{:S(2)}) collective-permute-start(f32[128,16]{0,1:T(8,128)S(1)} %get-tuple-element.23), channel_id=1, source_target_pairs={{0,3},{1,0},{2,1},{3,2},{4,7},{5,4},{6,5},{7,6},{8,11},{9,8},{10,9... | collective-permute-start | bytes 24584 | tf_op jit(solution)/shard_map/ppermute | solution.py:11
  47.4 12.0 %collective-permute-start.4 = (f32[128,16]{0,1:T(8,128)S(1)}, f32[128,16]{0,1:T(8,128)}, u32[]{:S(2)}, u32[]{:S(2)}) collective-permute-start(f32[128,16]{0,1:T(8,128)S(1)} %get-tuple-element.22), channel_id=1, source_target_pairs={{0,4},{4,8},{8,12},{12,16},{16,20},{20,24},{24,28},{28,0},{1,5},{5... | collective-permute-start | bytes 24584 | tf_op jit(solution)/shard_map/ppermute | solution.py:11
  51.5 9.1 %collective-permute-start.5 = (f32[128,16]{0,1:T(8,128)S(1)}, f32[128,16]{0,1:T(8,128)S(1)}, u32[]{:S(2)}, u32[]{:S(2)}) collective-permute-start(f32[128,16]{0,1:T(8,128)S(1)} %get-tuple-element.21), channel_id=1, source_target_pairs={{0,28},{4,0},{8,4},{12,8},{16,12},{20,16},{24,20},{28,24},{1,29},{... | collective-permute-start | bytes 24584 | tf_op jit(solution)/shard_map/ppermute | solution.py:11
  87.2 9.9 %collective-permute-start.6 = (f32[128,16]{0,1:T(8,128)S(1)}, f32[128,16]{0,1:T(8,128)S(1)}, u32[]{:S(2)}, u32[]{:S(2)}) collective-permute-start(f32[128,16]{0,1:T(8,128)S(1)} %get-tuple-element.20), channel_id=1, source_target_pairs={{0,1},{1,2},{2,3},{3,0},{4,5},{5,6},{6,7},{7,4},{8,9},{9,10},{10,1... | collective-permute-start | bytes 24584 | tf_op jit(solution)/shard_map/ppermute | solution.py:11
  89.5 10.3 %collective-permute-start.7 = (f32[128,16]{0,1:T(8,128)S(1)}, f32[128,16]{0,1:T(8,128)S(1)}, u32[]{:S(2)}, u32[]{:S(2)}) collective-permute-start(f32[128,16]{0,1:T(8,128)S(1)} %get-tuple-element.19), channel_id=1, source_target_pairs={{0,3},{1,0},{2,1},{3,2},{4,7},{5,4},{6,5},{7,6},{8,11},{9,8},{10,9... | collective-permute-start | bytes 24584 | tf_op jit(solution)/shard_map/ppermute | solution.py:11
  93.3 6.5 %collective-permute-start.8 = (f32[128,16]{0,1:T(8,128)S(1)}, f32[128,16]{0,1:T(8,128)S(1)}, u32[]{:S(2)}, u32[]{:S(2)}) collective-permute-start(f32[128,16]{0,1:T(8,128)S(1)} %get-tuple-element.18), channel_id=1, source_target_pairs={{0,1},{1,2},{2,3},{3,0},{4,5},{5,6},{6,7},{7,4},{8,9},{9,10},{10,1... | collective-permute-start | bytes 24584 | tf_op jit(solution)/shard_map/ppermute | solution.py:11
  93.3 6.5 %collective-permute-start.9 = (f32[128,16]{0,1:T(8,128)S(1)}, f32[128,16]{0,1:T(8,128)S(1)}, u32[]{:S(2)}, u32[]{:S(2)}) collective-permute-start(f32[128,16]{0,1:T(8,128)S(1)} %get-tuple-element.17), channel_id=1, source_target_pairs={{0,3},{1,0},{2,1},{3,2},{4,7},{5,4},{6,5},{7,6},{8,11},{9,8},{10,9... | collective-permute-start | bytes 24584 | tf_op jit(solution)/shard_map/ppermute | solution.py:11
  97.1 4.0 %collective-permute-start.10 = (f32[128,16]{0,1:T(8,128)S(1)}, f32[128,16]{0,1:T(8,128)S(1)}, u32[]{:S(2)}, u32[]{:S(2)}) collective-permute-start(f32[128,16]{0,1:T(8,128)S(1)} %get-tuple-element.16), channel_id=1, source_target_pairs={{0,4},{4,8},{8,12},{12,16},{16,20},{20,24},{24,28},{28,0},{1,5},{5... | collective-permute-start | bytes 24584 | tf_op jit(solution)/shard_map/ppermute | solution.py:11
  97.1 4.0 %collective-permute-start.11 = (f32[128,16]{0,1:T(8,128)S(1)}, f32[128,16]{0,1:T(8,128)S(1)}, u32[]{:S(2)}, u32[]{:S(2)}) collective-permute-start(f32[128,16]{0,1:T(8,128)S(1)} %get-tuple-element.15), channel_id=1, source_target_pairs={{0,28},{4,0},{8,4},{12,8},{16,12},{20,16},{24,20},{28,24},{1,29},{... | collective-permute-start | bytes 24584 | tf_op jit(solution)/shard_map/ppermute | solution.py:11
  126.4 9.3 %collective-permute-start.12 = (f32[128,16]{0,1:T(8,128)S(1)}, f32[128,16]{0,1:T(8,128)S(1)}, u32[]{:S(2)}, u32[]{:S(2)}) collective-permute-start(f32[128,16]{0,1:T(8,128)S(1)} %get-tuple-element.14), channel_id=1, source_target_pairs={{0,1},{1,2},{2,3},{3,0},{4,5},{5,6},{6,7},{7,4},{8,9},{9,10},{10,1... | collective-permute-start | bytes 24584 | tf_op jit(solution)/shard_map/ppermute | solution.py:11
  128.0 10.3 %collective-permute-start.13 = (f32[128,16]{0,1:T(8,128)S(1)}, f32[128,16]{0,1:T(8,128)S(1)}, u32[]{:S(2)}, u32[]{:S(2)}) collective-permute-start(f32[128,16]{0,1:T(8,128)S(1)} %get-tuple-element.13), channel_id=1, source_target_pairs={{0,3},{1,0},{2,1},{3,2},{4,7},{5,4},{6,5},{7,6},{8,11},{9,8},{10,9... | collective-permute-start | bytes 24584 | tf_op jit(solution)/shard_map/ppermute | solution.py:11
  131.9 6.5 %collective-permute-start.14 = (f32[128,16]{0,1:T(8,128)S(1)}, f32[128,16]{0,1:T(8,128)S(1)}, u32[]{:S(2)}, u32[]{:S(2)}) collective-permute-start(f32[128,16]{0,1:T(8,128)S(1)} %get-tuple-element.12), channel_id=1, source_target_pairs={{0,1},{1,2},{2,3},{3,0},{4,5},{5,6},{6,7},{7,4},{8,9},{9,10},{10,1... | collective-permute-start | bytes 24584 | tf_op jit(solution)/shard_map/ppermute | solution.py:11
  131.9 6.5 %collective-permute-start.15 = (f32[128,16]{0,1:T(8,128)S(1)}, f32[128,16]{0,1:T(8,128)S(1)}, u32[]{:S(2)}, u32[]{:S(2)}) collective-permute-start(f32[128,16]{0,1:T(8,128)S(1)} %get-tuple-element.11), channel_id=1, source_target_pairs={{0,3},{1,0},{2,1},{3,2},{4,7},{5,4},{6,5},{7,6},{8,11},{9,8},{10,9... | collective-permute-start | bytes 24584 | tf_op jit(solution)/shard_map/ppermute | solution.py:11
  135.7 4.0 %collective-permute-start.16 = (f32[128,16]{0,1:T(8,128)S(1)}, f32[128,16]{0,1:T(8,128)S(1)}, u32[]{:S(2)}, u32[]{:S(2)}) collective-permute-start(f32[128,16]{0,1:T(8,128)S(1)} %get-tuple-element.10), channel_id=1, source_target_pairs={{0,4},{4,8},{8,12},{12,16},{16,20},{20,24},{24,28},{28,0},{1,5},{5... | collective-permute-start | bytes 24584 | tf_op jit(solution)/shard_map/ppermute | solution.py:11
  135.7 4.0 %collective-permute-start.17 = (f32[128,16]{0,1:T(8,128)S(1)}, f32[128,16]{0,1:T(8,128)S(1)}, u32[]{:S(2)}, u32[]{:S(2)}) collective-permute-start(f32[128,16]{0,1:T(8,128)S(1)} %get-tuple-element.9), channel_id=1, source_target_pairs={{0,28},{4,0},{8,4},{12,8},{16,12},{20,16},{24,20},{28,24},{1,29},{... | collective-permute-start | bytes 24584 | tf_op jit(solution)/shard_map/ppermute | solution.py:11
  (10 other events, 109.0 us)
where the time goes:
time: 150 us; the launch traced here: 149 us
  local copies, waits for them, and re-layouts  48.4 us (32%)
  blocking collectives  38.5 us (26%)
  starting transfers between devices  34.5 us (23%)
  matrix products  20.4 us (14%)
  other arithmetic  3.46 us (2%)
  waiting for transfers between devices  2.68 us (2%)
    ppermute x18, starting transfers between devices, from_behind(): lax.ppermute(shard, axis, [(i, (i + by) % peers) for i in range(peers)])  31.1 us
    all_gather x3, blocking collectives, body(): lax.all_gather(local_coarse, 'sub', axis=0, tiled=True)  27.8 us
    gather x6, local copies, waits for them, and re-layouts, body(): permuted = jnp.take_along_axis(received, matched[:, :, None], axis=1)  24.4 us
    all_gather x1, blocking collectives, body(): every_ids = lax.all_gather(own_map, 'sub', axis=0, tiled=True)  10.7 us
    unnamed x47, local copies, waits for them, and re-layouts  8.21 us
    dot_general x3, matrix products, body(): jnp.einsum('tij,tjr->tir', tile_block, picked, preferred_element_type=jnp...  6.87 us
    gather x2, local copies, waits for them, and re-layouts, body(): jnp.take(inverse_rows, every_ids, axis=1)  5.21 us
    dot_general x3, matrix products, body(): jnp.einsum('bt,tir->bir', row_table, products, precision=lax.Precision.HI...  4.98 us
  transfers between devices with their start and end apart: 19, of which 2 were waited for; matrix products, arithmetic and copies ran while one was open for 11% of the time, Pallas kernels for 0%

commit v1 on v0

--- a/solution.py
+++ b/solution.py
@@ -41,7 +41,22 @@
     row_table = (listing[:, 0][None, :] == block_ids[:, None]).astype(jnp.float32)
     face_table = (faces_here[None, :] == block_ids[:, None]).astype(jnp.float32)
     stride = max(lax.axis_size("reg") // 4, 1)
-    every_ids = lax.all_gather(own_map, "sub", axis=0, tiled=True)
+    size, place, width = (lax.axis_size("sub"), lax.axis_index("sub"), own_map.shape[0])
+    forward = [(i_2, (i_2 + 1) % size) for i_2 in range(size)]
+    downward = [(i_2, (i_2 - 1) % size) for i_2 in range(size)]
+    out = jnp.zeros((*own_map.shape[:0], size * width, *own_map.shape[0 + 1 :]), own_map.dtype)
+    out = lax.dynamic_update_slice_in_dim(out, own_map, place * width, axis=0)
+    from_left = from_right = own_map
+    half = size // 2
+    for step in range(1, half + 1):
+        from_left = lax.ppermute(from_left, "sub", forward)
+        out = lax.dynamic_update_slice_in_dim(out, from_left, (place - step) % size * width, axis=0)
+        if step < size - half:
+            from_right = lax.ppermute(from_right, "sub", downward)
+            out = lax.dynamic_update_slice_in_dim(
+                out, from_right, (place + step) % size * width, axis=0
+            )
+    every_ids = out
     outgoing_part = jnp.take(inverse_rows, every_ids, axis=1).reshape(
         held_rows, lax.axis_size("sub"), own_count
     )

time: 150 us -> 156 us (1.040)
  blocking collectives: 38.5 us -> 27.7 us
  starting transfers between devices: 34.5 us -> 43.7 us
  waiting for transfers between devices: 2.68 us -> 6.79 us
  other arithmetic: 3.46 us -> 6.81 us
  matrix products: 20.4 us -> 22.9 us
  local copies, waits for them, and re-layouts: 48.4 us -> 46.1 us
    all_gather x1 -> x0, blocking collectives: 10.7 us -> none  [body(): every_ids = lax.all_gather(own_map, 'sub', axis=0, tiled=True)]
    ppermute x0 -> x7, starting transfers between devices: none -> 8.82 us  [the longest x3 8.27 us: body(): from_right = lax.ppermute(from_right, 'sub', downward)]
    ppermute x0 -> x7, waiting for transfers between devices: none -> 4.11 us  [the longest x4 3.93 us: body(): from_left = lax.ppermute(from_left, 'sub', forward)]
    gather x6, local copies, waits for them, and re-layouts: 24.4 us -> 21.6 us  [body(): permuted = jnp.take_along_axis(received, matched[:, :, None], axis=1)]
    gather x2, local copies, waits for them, and re-layouts: 5.21 us -> 2.99 us  [body(): jnp.take(inverse_rows, every_ids, axis=1)]
    dynamic_update_slice x0 -> x8, local copies, waits for them, and re-layouts: none -> 2.1 us  [the longest x1 0.77 us: body(): out = lax.dynamic_update_slice_in_dim(out, own_map, place * width, axis=0)]
    unnamed x47 -> x41, local copies, waits for them, and re-layouts: 8.21 us -> 8.18 us
  transfers between devices with their start and end apart: 19 -> 26, of which waited for: 2 -> 6; matrix products, arithmetic and copies ran while one was open for 11% -> 16% of each run, Pallas kernels for 0% -> 0%
where the time goes in v1:
time: 156 us; the launch traced here: 155 us
  local copies, waits for them, and re-layouts  46.1 us (30%)
  starting transfers between devices  43.7 us (28%)
  blocking collectives  27.7 us (18%)
  matrix products  22.9 us (15%)
  other arithmetic  6.81 us (4%)
  waiting for transfers between devices  6.79 us (4%)
    ppermute x18, starting transfers between devices, from_behind(): lax.ppermute(shard, axis, [(i, (i + by) % peers) for i in range(peers)])  31.4 us
    all_gather x3, blocking collectives, body(): lax.all_gather(local_coarse, 'sub', axis=0, tiled=True)  27.7 us
    gather x6, local copies, waits for them, and re-layouts, body(): permuted = jnp.take_along_axis(received, matched[:, :, None], axis=1)  21.6 us
    ppermute x3, starting transfers between devices, body(): from_right = lax.ppermute(from_right, 'sub', downward)  8.27 us
    unnamed x41, local copies, waits for them, and re-layouts  8.18 us
    dot_general x3, matrix products, body(): jnp.einsum('tij,tjr->tir', tile_block, picked, preferred_element_type=jnp...  6.91 us
    dot_general x3, matrix products, body(): jnp.einsum('bt,tir->bir', row_table, products, precision=lax.Precision.HI...  5.6 us
    dot_general x3, matrix products, body(): jnp.dot(own_block, lax.all_gather(local_coarse, 'sub', axis=0, tiled=True...  4.59 us
  transfers between devices with their start and end apart: 26, of which 6 were waited for; matrix products, arithmetic and copies ran while one was open for 16% of the time, Pallas kernels for 0%

profile of v1, /device:TPU:0, one launch (start us, length us, event | category | flops | bytes accessed | tf_op | source)
XLA Modules:
  0.0 155.2 jit_solution(9682849350432204065)
XLA Ops:
  1.2 2.9 %collective-permute-start.1 = (s32[128]{0:T(128)}, s32[128]{0:T(128)S(1)}, u32[]{:S(2)}, u32[]{:S(2)}) collective-permute-start(s32[128]{0:T(128)} %bitcast.268), channel_id=1, source_target_pairs={{0,28},{4,0},{8,4},{12,8},{16,12},{20,16},{24,20},{28,24},{1,29},{... | collective-permute-start | bytes 1544 | tf_op jit(solution)/shard_map/ppermute | solution.py:55
  11.8 2.6 %collective-permute-start.3 = (s32[128]{0:T(128)S(1)}, s32[128]{0:T(128)S(1)}, u32[]{:S(2)}, u32[]{:S(2)}) collective-permute-start(s32[128]{0:T(128)S(1)} %collective-permute-done.1), channel_id=1, source_target_pairs={{0,28},{4,0},{8,4},{12,8},{16,12},{20,16},{24,20},{28,24},{1,29},{... | collective-permute-start | bytes 1544 | tf_op jit(solution)/shard_map/ppermute | solution.py:55
  16.8 2.7 %collective-permute-start.5 = (s32[128]{0:T(128)S(1)}, s32[128]{0:T(128)S(1)}, u32[]{:S(2)}, u32[]{:S(2)}) collective-permute-start(s32[128]{0:T(128)S(1)} %collective-permute-done.3), channel_id=1, source_target_pairs={{0,28},{4,0},{8,4},{12,8},{16,12},{20,16},{24,20},{28,24},{1,29},{... | collective-permute-start | bytes 1544 | tf_op jit(solution)/shard_map/ppermute | solution.py:55
  20.9 2.6 %collective-permute-done.6 = s32[128]{0:T(128)S(1)} collective-permute-done((s32[128]{0:T(128)S(1)}, s32[128]{0:T(128)S(1)}, u32[]{:S(2)}, u32[]{:S(2)}) %collective-permute-start.6) | collective-permute-done | bytes 544 | tf_op jit(solution)/shard_map/ppermute | solution.py:52
  23.7 2.8 %gather_fusion = f32[1024,64]{1,0:T(8,128)S(1)} fusion(f32[64,512]{0,1:T(8,128)S(1)} %bitcast.252, s32[1024]{0:T(1024)S(1)} %fusion.82), kind=kCustom, calls=%fused_computation.9 | custom fusion | bytes 528384 | tf_op jit(solution)/shard_map/jit(_take)/gather | solution.py:60
  27.4 3.5 %all-to-all-start = ((f32[64,8,128]{2,0,1:T(8,128)}), f32[64,8,128]{2,0,1:T(8,128)S(1)}, u32[]{:S(2)}, u32[]{:S(2)}) async-start(f32[64,8,128]{2,0,1:T(8,128)} %broadcast_select_fusion), calls=%async_computation | async-start | bytes 524288 | tf_op jit(solution)/shard_map/all_to_all | solution.py:63
  30.9 10.3 %all_gather.9 = f32[1024,16]{0,1:T(8,128)S(1)} all-gather(f32[128,16]{0,1:T(8,128)S(1)} %fusion.37), channel_id=1, replica_groups=mesh['sub'=8,'reg'=4] {'sub'}, dimensions={0}, use_global_device_ids=true | all-gather | bytes 73728 | tf_op jit(solution)/shard_map/all_gather | solution.py:73
  41.2 4.0 %gather_fusion.1 = f32[1024,128]{1,0:T(8,128)} fusion(f32[512,128]{1,0:T(8,128)S(1)} %bitcast.251, s32[1024]{0:T(1024)S(1)} %fusion.82), kind=kCustom, calls=%fused_computation.10 | custom fusion | bytes 1052672 | tf_op jit(solution)/shard_map/jit(_take)/gather | solution.py:65
  52.0 3.8 %collective-permute-start.10 = (f32[128,16]{0,1:T(8,128)S(1)}, f32[128,16]{0,1:T(8,128)}, u32[]{:S(2)}, u32[]{:S(2)}) collective-permute-start(f32[128,16]{0,1:T(8,128)S(1)} %get-tuple-element.23), channel_id=1, source_target_pairs={{0,3},{1,0},{2,1},{3,2},{4,7},{5,4},{6,5},{7,6},{8,11},{9,8},{10,9... | collective-permute-start | bytes 24584 | tf_op jit(solution)/shard_map/ppermute | solution.py:11
  59.9 2.6 %collective-permute-start.12 = (f32[128,16]{0,1:T(8,128)S(1)}, f32[128,16]{0,1:T(8,128)S(1)}, u32[]{:S(2)}, u32[]{:S(2)}) collective-permute-start(f32[128,16]{0,1:T(8,128)S(1)} %get-tuple-element.21), channel_id=1, source_target_pairs={{0,28},{4,0},{8,4},{12,8},{16,12},{20,16},{24,20},{28,24},{1,29},{... | collective-permute-start | bytes 24584 | tf_op jit(solution)/shard_map/ppermute | solution.py:11
  70.6 7.0 %gather_fusion.4 = f32[768,16]{1,0:T(8,128)} fusion(f32[6,128,16]{2,1,0:T(8,128)S(1)} %copy.35, s32[768]{0:T(1024)S(1)} %bitcast.247), kind=kCustom, calls=%fused_computation.2.clone | custom fusion | bytes 104448 | tf_op jit(solution)/shard_map/jit(take_along_axis)/gather | solution.py:94
  80.2 8.4 %all_gather.10 = f32[1024,16]{0,1:T(8,128)S(1)} all-gather(f32[128,16]{0,1:T(8,128)S(1)} %convolution_bitcast_fusion.4), channel_id=1, replica_groups=mesh['sub'=8,'reg'=4] {'sub'}, dimensions={0}, use_global_device_ids=true | all-gather | bytes 73728 | tf_op jit(solution)/shard_map/all_gather | solution.py:73
  91.9 2.4 %fusion.14 = f32[80,128,16]{1,2,0:T(8,128)} fusion(bf16[1,1,80,128,128]{4,3,2,1,0:T(8,128)(2,1)S(1)} %copy-done, bf16[80,128,16]{1,2,0:T(8,128)(2,1)S(1)} %gather_fusion.5, pred[80]{0:T(512)(128)(4,1)S(1)} %copy-done.11), kind=kOutput, calls=%fused_computation.26 | convolution fusion | flops 42106880 | bytes 3604560 | tf_op jit(solution)/shard_map/tij,tjr->tir/dot_general | solution.py:82
  97.2 3.8 %collective-permute-start.14 = (f32[128,16]{0,1:T(8,128)S(1)}, f32[128,16]{0,1:T(8,128)S(1)}, u32[]{:S(2)}, u32[]{:S(2)}) collective-permute-start(f32[128,16]{0,1:T(8,128)S(1)} %get-tuple-element.19), channel_id=1, source_target_pairs={{0,3},{1,0},{2,1},{3,2},{4,7},{5,4},{6,5},{7,6},{8,11},{9,8},{10,9... | collective-permute-start | bytes 24584 | tf_op jit(solution)/shard_map/ppermute | solution.py:11
  101.0 3.8 %collective-permute-start.16 = (f32[128,16]{0,1:T(8,128)S(1)}, f32[128,16]{0,1:T(8,128)S(1)}, u32[]{:S(2)}, u32[]{:S(2)}) collective-permute-start(f32[128,16]{0,1:T(8,128)S(1)} %get-tuple-element.17), channel_id=1, source_target_pairs={{0,3},{1,0},{2,1},{3,2},{4,7},{5,4},{6,5},{7,6},{8,11},{9,8},{10,9... | collective-permute-start | bytes 24584 | tf_op jit(solution)/shard_map/ppermute | solution.py:11
  104.8 2.6 %collective-permute-start.18 = (f32[128,16]{0,1:T(8,128)S(1)}, f32[128,16]{0,1:T(8,128)S(1)}, u32[]{:S(2)}, u32[]{:S(2)}) collective-permute-start(f32[128,16]{0,1:T(8,128)S(1)} %get-tuple-element.15), channel_id=1, source_target_pairs={{0,28},{4,0},{8,4},{12,8},{16,12},{20,16},{24,20},{28,24},{1,29},{... | collective-permute-start | bytes 24584 | tf_op jit(solution)/shard_map/ppermute | solution.py:11
  109.0 7.0 %gather_fusion.7 = f32[768,16]{1,0:T(8,128)} fusion(f32[6,128,16]{2,1,0:T(8,128)S(1)} %copy.40, s32[768]{0:T(1024)S(1)} %bitcast.248), kind=kCustom, calls=%fused_computation.7.clone | custom fusion | bytes 104448 | tf_op jit(solution)/shard_map/jit(take_along_axis)/gather | solution.py:94
  118.6 9.1 %all_gather.11 = f32[1024,16]{0,1:T(8,128)S(1)} all-gather(f32[128,16]{0,1:T(8,128)S(1)} %convolution_bitcast_fusion.3), channel_id=1, replica_groups=mesh['sub'=8,'reg'=4] {'sub'}, dimensions={0}, use_global_device_ids=true | all-gather | bytes 73728 | tf_op jit(solution)/shard_map/all_gather | solution.py:73
  130.9 2.4 %fusion.17 = f32[80,128,16]{1,2,0:T(8,128)} fusion(bf16[1,1,80,128,128]{4,3,2,1,0:T(8,128)(2,1)S(1)} %copy-done, bf16[80,128,16]{1,2,0:T(8,128)(2,1)S(1)} %gather_fusion.8, pred[80]{0:T(512)(128)(4,1)S(1)} %copy-done.11), kind=kOutput, calls=%fused_computation.27 | convolution fusion | flops 42106880 | bytes 3604560 | tf_op jit(solution)/shard_map/tij,tjr->tir/dot_general | solution.py:82
  134.0 2.2 %fusion.23 = f32[10,128,16]{1,0,2:T(8,128)} fusion(f32[80,128,16]{1,2,0:T(8,128)} %fusion.17, s32[80]{0:T(128)S(1)} %copy-done.10), kind=kOutput, calls=%fused_computation.39 | convolution fusion | flops 19661600 | bytes 737600 | tf_op jit(solution)/shard_map/bt,tir->bir/dot_general | solution.py:85
  136.2 3.8 %collective-permute-start.20 = (f32[128,16]{0,1:T(8,128)S(1)}, f32[128,16]{0,1:T(8,128)S(1)}, u32[]{:S(2)}, u32[]{:S(2)}) collective-permute-start(f32[128,16]{0,1:T(8,128)S(1)} %get-tuple-element.13), channel_id=1, source_target_pairs={{0,3},{1,0},{2,1},{3,2},{4,7},{5,4},{6,5},{7,6},{8,11},{9,8},{10,9... | collective-permute-start | bytes 24584 | tf_op jit(solution)/shard_map/ppermute | solution.py:11
  140.0 3.8 %collective-permute-start.22 = (f32[128,16]{0,1:T(8,128)S(1)}, f32[128,16]{0,1:T(8,128)S(1)}, u32[]{:S(2)}, u32[]{:S(2)}) collective-permute-start(f32[128,16]{0,1:T(8,128)S(1)} %get-tuple-element.11), channel_id=1, source_target_pairs={{0,3},{1,0},{2,1},{3,2},{4,7},{5,4},{6,5},{7,6},{8,11},{9,8},{10,9... | collective-permute-start | bytes 24584 | tf_op jit(solution)/shard_map/ppermute | solution.py:11
  143.8 2.6 %collective-permute-start.24 = (f32[128,16]{0,1:T(8,128)S(1)}, f32[128,16]{0,1:T(8,128)S(1)}, u32[]{:S(2)}, u32[]{:S(2)}) collective-permute-start(f32[128,16]{0,1:T(8,128)S(1)} %get-tuple-element.9), channel_id=1, source_target_pairs={{0,28},{4,0},{8,4},{12,8},{16,12},{20,16},{24,20},{28,24},{1,29},{... | collective-permute-start | bytes 24584 | tf_op jit(solution)/shard_map/ppermute | solution.py:11
  148.0 5.1 %gather_fusion.10 = f32[768,16]{1,0:T(8,128)S(1)} fusion(f32[6,128,16]{2,1,0:T(8,128)S(1)} %copy.45, s32[768]{0:T(1024)S(1)} %bitcast.249), kind=kCustom, calls=%fused_computation.8.clone | custom fusion | bytes 104448 | tf_op jit(solution)/shard_map/jit(take_along_axis)/gather | solution.py:94
  (149 shorter events, 52.2 us)
Async XLA Ops:
  0.6 11.2 %collective-permute-start = (s32[128]{0:T(128)}, s32[128]{0:T(128)S(1)}, u32[]{:S(2)}, u32[]{:S(2)}) collective-permute-start(s32[128]{0:T(128)} %bitcast.267), channel_id=1, source_target_pairs={{0,4},{4,8},{8,12},{12,16},{16,20},{20,24},{24,28},{28,0},{1,5},{5... | collective-permute-start | bytes 1544 | tf_op jit(solution)/shard_map/ppermute | solution.py:52
  1.2 10.6 %collective-permute-start.1 = (s32[128]{0:T(128)}, s32[128]{0:T(128)S(1)}, u32[]{:S(2)}, u32[]{:S(2)}) collective-permute-start(s32[128]{0:T(128)} %bitcast.268), channel_id=1, source_target_pairs={{0,28},{4,0},{8,4},{12,8},{16,12},{20,16},{24,20},{28,24},{1,29},{... | collective-permute-start | bytes 1544 | tf_op jit(solution)/shard_map/ppermute | solution.py:55
  11.8 3.9 %collective-permute-start.2 = (s32[128]{0:T(128)S(1)}, s32[128]{0:T(128)S(1)}, u32[]{:S(2)}, u32[]{:S(2)}) collective-permute-start(s32[128]{0:T(128)S(1)} %collective-permute-done), channel_id=1, source_target_pairs={{0,4},{4,8},{8,12},{12,16},{16,20},{20,24},{24,28},{28,0},{1,5},{5... | collective-permute-start | bytes 1544 | tf_op jit(solution)/shard_map/ppermute | solution.py:52
  11.8 4.9 %collective-permute-start.3 = (s32[128]{0:T(128)S(1)}, s32[128]{0:T(128)S(1)}, u32[]{:S(2)}, u32[]{:S(2)}) collective-permute-start(s32[128]{0:T(128)S(1)} %collective-permute-done.1), channel_id=1, source_target_pairs={{0,28},{4,0},{8,4},{12,8},{16,12},{20,16},{24,20},{28,24},{1,29},{... | collective-permute-start | bytes 1544 | tf_op jit(solution)/shard_map/ppermute | solution.py:55
  16.8 4.0 %collective-permute-start.5 = (s32[128]{0:T(128)S(1)}, s32[128]{0:T(128)S(1)}, u32[]{:S(2)}, u32[]{:S(2)}) collective-permute-start(s32[128]{0:T(128)S(1)} %collective-permute-done.3), channel_id=1, source_target_pairs={{0,28},{4,0},{8,4},{12,8},{16,12},{20,16},{24,20},{28,24},{1,29},{... | collective-permute-start | bytes 1544 | tf_op jit(solution)/shard_map/ppermute | solution.py:55
  27.4 13.8 %all-to-all-start = ((f32[64,8,128]{2,0,1:T(8,128)}), f32[64,8,128]{2,0,1:T(8,128)S(1)}, u32[]{:S(2)}, u32[]{:S(2)}) async-start(f32[64,8,128]{2,0,1:T(8,128)} %broadcast_select_fusion), calls=%async_computation | async-start | bytes 524288 | tf_op jit(solution)/shard_map/all_to_all | solution.py:63
  47.7 12.2 %collective-permute-start.7 = (f32[128,16]{0,1:T(8,128)S(1)}, f32[128,16]{0,1:T(8,128)}, u32[]{:S(2)}, u32[]{:S(2)}) collective-permute-start(f32[128,16]{0,1:T(8,128)S(1)} %get-tuple-element.26), channel_id=1, source_target_pairs={{0,1},{1,2},{2,3},{3,0},{4,5},{5,6},{6,7},{7,4},{8,9},{9,10},{10,1... | collective-permute-start | bytes 24584 | tf_op jit(solution)/shard_map/ppermute | solution.py:11
  49.9 14.0 %collective-permute-start.8 = (f32[128,16]{0,1:T(8,128)S(1)}, f32[128,16]{0,1:T(8,128)}, u32[]{:S(2)}, u32[]{:S(2)}) collective-permute-start(f32[128,16]{0,1:T(8,128)S(1)} %get-tuple-element.25), channel_id=1, source_target_pairs={{0,3},{1,0},{2,1},{3,2},{4,7},{5,4},{6,5},{7,6},{8,11},{9,8},{10,9... | collective-permute-start | bytes 24584 | tf_op jit(solution)/shard_map/ppermute | solution.py:11
  51.9 13.2 %collective-permute-start.9 = (f32[128,16]{0,1:T(8,128)S(1)}, f32[128,16]{0,1:T(8,128)}, u32[]{:S(2)}, u32[]{:S(2)}) collective-permute-start(f32[128,16]{0,1:T(8,128)S(1)} %get-tuple-element.24), channel_id=1, source_target_pairs={{0,1},{1,2},{2,3},{3,0},{4,5},{5,6},{6,7},{7,4},{8,9},{9,10},{10,1... | collective-permute-start | bytes 24584 | tf_op jit(solution)/shard_map/ppermute | solution.py:11
  52.0 14.5 %collective-permute-start.10 = (f32[128,16]{0,1:T(8,128)S(1)}, f32[128,16]{0,1:T(8,128)}, u32[]{:S(2)}, u32[]{:S(2)}) collective-permute-start(f32[128,16]{0,1:T(8,128)S(1)} %get-tuple-element.23), channel_id=1, source_target_pairs={{0,3},{1,0},{2,1},{3,2},{4,7},{5,4},{6,5},{7,6},{8,11},{9,8},{10,9... | collective-permute-start | bytes 24584 | tf_op jit(solution)/shard_map/ppermute | solution.py:11
  55.8 11.9 %collective-permute-start.11 = (f32[128,16]{0,1:T(8,128)S(1)}, f32[128,16]{0,1:T(8,128)}, u32[]{:S(2)}, u32[]{:S(2)}) collective-permute-start(f32[128,16]{0,1:T(8,128)S(1)} %get-tuple-element.22), channel_id=1, source_target_pairs={{0,4},{4,8},{8,12},{12,16},{16,20},{20,24},{24,28},{28,0},{1,5},{5... | collective-permute-start | bytes 24584 | tf_op jit(solution)/shard_map/ppermute | solution.py:11
  59.9 9.1 %collective-permute-start.12 = (f32[128,16]{0,1:T(8,128)S(1)}, f32[128,16]{0,1:T(8,128)S(1)}, u32[]{:S(2)}, u32[]{:S(2)}) collective-permute-start(f32[128,16]{0,1:T(8,128)S(1)} %get-tuple-element.21), channel_id=1, source_target_pairs={{0,28},{4,0},{8,4},{12,8},{16,12},{20,16},{24,20},{28,24},{1,29},{... | collective-permute-start | bytes 24584 | tf_op jit(solution)/shard_map/ppermute | solution.py:11
  94.9 9.9 %collective-permute-start.13 = (f32[128,16]{0,1:T(8,128)S(1)}, f32[128,16]{0,1:T(8,128)S(1)}, u32[]{:S(2)}, u32[]{:S(2)}) collective-permute-start(f32[128,16]{0,1:T(8,128)S(1)} %get-tuple-element.20), channel_id=1, source_target_pairs={{0,1},{1,2},{2,3},{3,0},{4,5},{5,6},{6,7},{7,4},{8,9},{9,10},{10,1... | collective-permute-start | bytes 24584 | tf_op jit(solution)/shard_map/ppermute | solution.py:11
  97.2 10.3 %collective-permute-start.14 = (f32[128,16]{0,1:T(8,128)S(1)}, f32[128,16]{0,1:T(8,128)S(1)}, u32[]{:S(2)}, u32[]{:S(2)}) collective-permute-start(f32[128,16]{0,1:T(8,128)S(1)} %get-tuple-element.19), channel_id=1, source_target_pairs={{0,3},{1,0},{2,1},{3,2},{4,7},{5,4},{6,5},{7,6},{8,11},{9,8},{10,9... | collective-permute-start | bytes 24584 | tf_op jit(solution)/shard_map/ppermute | solution.py:11
  101.0 6.5 %collective-permute-start.15 = (f32[128,16]{0,1:T(8,128)S(1)}, f32[128,16]{0,1:T(8,128)S(1)}, u32[]{:S(2)}, u32[]{:S(2)}) collective-permute-start(f32[128,16]{0,1:T(8,128)S(1)} %get-tuple-element.18), channel_id=1, source_target_pairs={{0,1},{1,2},{2,3},{3,0},{4,5},{5,6},{6,7},{7,4},{8,9},{9,10},{10,1... | collective-permute-start | bytes 24584 | tf_op jit(solution)/shard_map/ppermute | solution.py:11
  101.0 6.5 %collective-permute-start.16 = (f32[128,16]{0,1:T(8,128)S(1)}, f32[128,16]{0,1:T(8,128)S(1)}, u32[]{:S(2)}, u32[]{:S(2)}) collective-permute-start(f32[128,16]{0,1:T(8,128)S(1)} %get-tuple-element.17), channel_id=1, source_target_pairs={{0,3},{1,0},{2,1},{3,2},{4,7},{5,4},{6,5},{7,6},{8,11},{9,8},{10,9... | collective-permute-start | bytes 24584 | tf_op jit(solution)/shard_map/ppermute | solution.py:11
  104.8 4.0 %collective-permute-start.17 = (f32[128,16]{0,1:T(8,128)S(1)}, f32[128,16]{0,1:T(8,128)S(1)}, u32[]{:S(2)}, u32[]{:S(2)}) collective-permute-start(f32[128,16]{0,1:T(8,128)S(1)} %get-tuple-element.16), channel_id=1, source_target_pairs={{0,4},{4,8},{8,12},{12,16},{16,20},{20,24},{24,28},{28,0},{1,5},{5... | collective-permute-start | bytes 24584 | tf_op jit(solution)/shard_map/ppermute | solution.py:11
  104.8 4.0 %collective-permute-start.18 = (f32[128,16]{0,1:T(8,128)S(1)}, f32[128,16]{0,1:T(8,128)S(1)}, u32[]{:S(2)}, u32[]{:S(2)}) collective-permute-start(f32[128,16]{0,1:T(8,128)S(1)} %get-tuple-element.15), channel_id=1, source_target_pairs={{0,28},{4,0},{8,4},{12,8},{16,12},{20,16},{24,20},{28,24},{1,29},{... | collective-permute-start | bytes 24584 | tf_op jit(solution)/shard_map/ppermute | solution.py:11
  133.9 9.9 %collective-permute-start.19 = (f32[128,16]{0,1:T(8,128)S(1)}, f32[128,16]{0,1:T(8,128)S(1)}, u32[]{:S(2)}, u32[]{:S(2)}) collective-permute-start(f32[128,16]{0,1:T(8,128)S(1)} %get-tuple-element.14), channel_id=1, source_target_pairs={{0,1},{1,2},{2,3},{3,0},{4,5},{5,6},{6,7},{7,4},{8,9},{9,10},{10,1... | collective-permute-start | bytes 24584 | tf_op jit(solution)/shard_map/ppermute | solution.py:11
  136.2 10.3 %collective-permute-start.20 = (f32[128,16]{0,1:T(8,128)S(1)}, f32[128,16]{0,1:T(8,128)S(1)}, u32[]{:S(2)}, u32[]{:S(2)}) collective-permute-start(f32[128,16]{0,1:T(8,128)S(1)} %get-tuple-element.13), channel_id=1, source_target_pairs={{0,3},{1,0},{2,1},{3,2},{4,7},{5,4},{6,5},{7,6},{8,11},{9,8},{10,9... | collective-permute-start | bytes 24584 | tf_op jit(solution)/shard_map/ppermute | solution.py:11
  140.0 6.5 %collective-permute-start.21 = (f32[128,16]{0,1:T(8,128)S(1)}, f32[128,16]{0,1:T(8,128)S(1)}, u32[]{:S(2)}, u32[]{:S(2)}) collective-permute-start(f32[128,16]{0,1:T(8,128)S(1)} %get-tuple-element.12), channel_id=1, source_target_pairs={{0,1},{1,2},{2,3},{3,0},{4,5},{5,6},{6,7},{7,4},{8,9},{9,10},{10,1... | collective-permute-start | bytes 24584 | tf_op jit(solution)/shard_map/ppermute | solution.py:11
  140.0 6.5 %collective-permute-start.22 = (f32[128,16]{0,1:T(8,128)S(1)}, f32[128,16]{0,1:T(8,128)S(1)}, u32[]{:S(2)}, u32[]{:S(2)}) collective-permute-start(f32[128,16]{0,1:T(8,128)S(1)} %get-tuple-element.11), channel_id=1, source_target_pairs={{0,3},{1,0},{2,1},{3,2},{4,7},{5,4},{6,5},{7,6},{8,11},{9,8},{10,9... | collective-permute-start | bytes 24584 | tf_op jit(solution)/shard_map/ppermute | solution.py:11
  143.8 4.0 %collective-permute-start.23 = (f32[128,16]{0,1:T(8,128)S(1)}, f32[128,16]{0,1:T(8,128)S(1)}, u32[]{:S(2)}, u32[]{:S(2)}) collective-permute-start(f32[128,16]{0,1:T(8,128)S(1)} %get-tuple-element.10), channel_id=1, source_target_pairs={{0,4},{4,8},{8,12},{12,16},{16,20},{20,24},{24,28},{28,0},{1,5},{5... | collective-permute-start | bytes 24584 | tf_op jit(solution)/shard_map/ppermute | solution.py:11
  143.8 4.0 %collective-permute-start.24 = (f32[128,16]{0,1:T(8,128)S(1)}, f32[128,16]{0,1:T(8,128)S(1)}, u32[]{:S(2)}, u32[]{:S(2)}) collective-permute-start(f32[128,16]{0,1:T(8,128)S(1)} %get-tuple-element.9), channel_id=1, source_target_pairs={{0,28},{4,0},{8,4},{12,8},{16,12},{20,16},{24,20},{28,24},{1,29},{... | collective-permute-start | bytes 24584 | tf_op jit(solution)/shard_map/ppermute | solution.py:11
  (14 other events, 200.4 us)
